TPU v7x, 128 devices: a whole 4x4x4 slice. The times are simulated.
128 devices in a mesh: row: 16 (over z_lo, y, core), col: 8 (over x, z_hi).
Axes of the slice: x: 4, y: 4, z: 4 (z_hi: 2, z_lo: 2; z = z_hi * 2 + z_lo), core: 2. Of those that a mesh axis runs over, the one named last changes fastest.
Arguments:
- queries: bfloat16 [8, 128, 4096], P(None, 'row', 'col'), may hold values from -13 to 13, as said below
- key_cache: bfloat16 [8, 65536, 1024], P(None, ('row', 'col')), may hold values from -13 to 13
- value_cache: bfloat16 [8, 65536, 1024], P(None, ('row', 'col')), may hold values from -6 to 6
- key_table: bfloat16 [1024, 1024], replicated, may hold values from -24 to 24
- value_table: bfloat16 [1024, 1024], replicated, may hold values from -6 to 6
- lengths: int32 [8], replicated, may hold values from 8192 to 65536
- token_ids: int32 [8, 128], P(None, 'row'), may hold values from 0 to 1023
Outputs:
- attended: bfloat16 [8, 128, 4096], P(None, 'row', 'col')
Inputs may be any that keep to these rules, and one draw needn't show every extreme that they name: `queries`: entries of the query array lie in the stated range.
All inputs are finite; a program needn't handle non-finite values.
Results may differ from a plain program's by a relative error of at most 0.006.
Values may be sent and summed in bfloat16 or wider, within the bound.
No kernel may reach another device: no remote copies, remote signals or barrier semaphores. Data moves between devices by JAX's collectives and lax.ppermute only.
A program may use at most 192 MiB of HBM per device.

v0:
```python
import jax
import jax.numpy as jnp
from jax import lax
from jax.sharding import PartitionSpec as P

HQ = 32
KH = 8
HD = 128


def laid_out(tiles, dim):
    lengths = list(tiles.shape[1:])
    lengths[dim] *= tiles.shape[0]
    return jnp.moveaxis(tiles, 0, dim).reshape(lengths)


def copy_for_each(array, axis):
    count = lax.axis_size(axis)
    return lax.all_to_all(
        jnp.broadcast_to(array[None], (count, *array.shape)), axis, 0, 0, tiled=True
    )


def gathered_copies(array, axis, dim):
    return laid_out(copy_for_each(array, axis), dim)


def cache_partials(whole, key_cache, value_cache, lengths, offset):
    users, beams, width = whole.shape
    positions = key_cache.shape[1]
    group = HQ // KH
    scale = HD ** (-0.5)

    def one_user(items):
        q_user, k_user, v_user, limit = items
        q_heads = q_user.reshape(beams, KH, group, HD)
        k_heads = k_user.reshape(positions, KH, HD)
        v_heads = v_user.reshape(positions, KH, HD)
        s = (
            jnp.einsum("wkgd,lkd->kwgl", q_heads, k_heads, preferred_element_type=jnp.float32)
            * scale
        )
        live = offset + jnp.arange(positions, dtype=jnp.int32) < limit
        s = jnp.where(live, s, -1e30)
        peak = jnp.max(s, axis=-1)
        weight = jnp.where(live, jnp.exp(s - peak[..., None]), 0.0)
        total = jnp.sum(weight, axis=-1)
        numer = jnp.einsum(
            "kwgl,lkd->wkgd",
            weight.astype(jnp.bfloat16),
            v_heads,
            preferred_element_type=jnp.float32,
        )
        peak = jnp.transpose(peak, (1, 0, 2)).reshape(beams, HQ)
        total = jnp.transpose(total, (1, 0, 2)).reshape(beams, HQ)
        return (numer.reshape(beams, width), peak, total)

    return lax.map(one_user, (whole, key_cache, value_cache, lengths))


def body(queries, key_cache, value_cache, key_table, value_table, lengths, token_ids):
    users, beam_part, width_part = queries.shape
    heads_part = width_part // HD
    scale = HD ** (-0.5)
    row_at = lax.axis_index("row")
    col_at = lax.axis_index("col")
    whole = gathered_copies(queries, "col", 2)
    whole = lax.all_gather(whole, "row", axis=1, tiled=True)
    offset = (row_at * lax.axis_size("col") + col_at) * key_cache.shape[1]
    numer_part, peak_part, total_part = cache_partials(
        whole, key_cache, value_cache, lengths, offset
    )
    peak_all = lax.pmax(peak_part, ("row", "col"))
    factor = jnp.exp(peak_part - peak_all)
    weighted = (numer_part.reshape(users, -1, HQ, HD) * factor[..., None]).reshape(
        users, -1, HQ * HD
    )
    mass = total_part * factor

    def local_part(array, per_head):
        picked = lax.dynamic_slice_in_dim(array, row_at * beam_part, beam_part, 1)
        return lax.dynamic_slice_in_dim(
            picked, col_at * heads_part * per_head, heads_part * per_head, 2
        )

    numer, total = lax.psum((weighted, mass), ("row", "col"))
    numer = local_part(numer, HD)
    total = local_part(total, 1)
    peak = local_part(peak_all, 1)
    codes = jnp.arange(key_table.shape[0], dtype=jnp.int32)
    onehot = (token_ids[..., None] == codes).astype(jnp.bfloat16)
    own_keys = jnp.einsum("uwv,vc->uwc", onehot, key_table, preferred_element_type=jnp.float32)
    own_values = jnp.einsum("uwv,vc->uwc", onehot, value_table, preferred_element_type=jnp.float32)
    group = HQ // KH
    own_keys = jnp.repeat(own_keys.reshape(users, beam_part, KH, HD), group, axis=2)
    own_values = jnp.repeat(own_values.reshape(users, beam_part, KH, HD), group, axis=2)
    own_keys = lax.dynamic_slice_in_dim(own_keys, col_at * heads_part, heads_part, 2)
    own_values = lax.dynamic_slice_in_dim(own_values, col_at * heads_part, heads_part, 2)
    q_local = queries.astype(jnp.float32).reshape(users, beam_part, heads_part, HD)
    own_score = jnp.sum(q_local * own_keys, axis=-1) * scale
    final_peak = jnp.maximum(peak, own_score)
    carried = jnp.exp(peak - final_peak)
    fresh = jnp.exp(own_score - final_peak)
    numer = (
        numer.reshape(users, beam_part, heads_part, HD) * carried[..., None]
        + fresh[..., None] * own_values
    )
    total = total * carried + fresh
    result = numer / total[..., None]
    return result.reshape(users, beam_part, width_part).astype(jnp.bfloat16)


def solution(mesh):
    return jax.shard_map(
        body,
        mesh=mesh,
        in_specs=(
            P(None, "row", "col"),
            P(None, ("row", "col"), None),
            P(None, ("row", "col"), None),
            P(),
            P(),
            P(),
            P(None, "row"),
        ),
        out_specs=P(None, "row", "col"),
        check_vma=False,
    )
```

profile of v0, /device:TPU:1, one launch (start us, length us, event | category | flops | bytes accessed | tf_op | source)
XLA Modules:
  0.0 743.7 jit_solution(7798961752427165654)
XLA Ops:
  7.6 17.5 %all_to_all.5 = bf16[8,8,8,512]{3,2,1,0:T(8,128)(2,1)S(1)} all-to-all(bf16[8,8,8,512]{3,2,1,0:T(8,128)(2,1)S(1)} %broadcast_in_dim.46), channel_id=1, replica_groups=mesh['row'=16,'col'=8] {'col'}, dimensions={0} | all-to-all | bytes 1048576 | tf_op jit(solution)/shard_map/all_to_all | solution.py:19
  26.6 52.4 %all-gather.2.cloned.1.call-done = bf16[8,128,4096]{2,0,1:T(8,128)(2,1)} async-done(((bf16[8,8,4096]{2,0,1:T(8,128)(2,1)}), bf16[8,128,4096]{2,0,1:T(8,128)(2,1)}) %all-gather.2.cloned.1.call-update) | async-done | bytes 8388624 | tf_op jit(solution)/shard_map/all_gather | solution.py:68
  79.0 12.5 %copy.35 = bf16[8,128,4096]{1,2,0:T(8,128)(2,1)} copy(bf16[8,128,4096]{2,0,1:T(8,128)(2,1)} %all-gather.2.cloned.1.call-done) | data formatting | bytes 16777216 | tf_op jit(solution)/shard_map/while | solution.py:58
  91.5 240.9 %while.14 = (s32[]{:T(128)}, f32[8,128,4096]{2,1,0:T(8,128)}, f32[8,128,32]{1,2,0:T(8,128)}, f32[8,128,32]{1,2,0:T(8,128)S(1)}, bf16[8,512,1024]{2,1,0:T(8,128)(...) while((s32[]{:T(128)}, f32[8,128,4096]{2,1,0:T(8,128)}, ...), condition=%wide.region_3.4_spmd, body=%wide.region_0.3_spmd.sunk | while | flops 1100997632 | bytes 82971808 | solution.py:58
  99.6 3.2 copy-done.1
  108.4 7.2 fusion.46
  118.5 3.1 constant_dynamic-update-slice_fusion.2
  129.7 3.2 copy-done.1
  138.5 7.2 fusion.46
  159.8 3.2 copy-done.1
  168.6 7.2 fusion.46
  178.7 3.1 constant_dynamic-update-slice_fusion.2
  189.9 3.2 copy-done.1
  198.7 7.2 fusion.46
  208.8 3.1 constant_dynamic-update-slice_fusion.2
  220.0 3.2 copy-done.1
  228.8 7.2 fusion.46
  238.9 3.1 constant_dynamic-update-slice_fusion.2
  250.1 3.2 copy-done.1
  258.9 7.2 fusion.46
  269.0 3.1 constant_dynamic-update-slice_fusion.2
  280.3 3.2 copy-done.1
  289.0 7.2 fusion.46
  299.1 3.1 constant_dynamic-update-slice_fusion.2
  310.4 3.2 copy-done.1
  319.2 7.2 fusion.46
  329.3 3.1 constant_dynamic-update-slice_fusion.2
  332.5 140.7 %all-reduce.4.cloned.1.call-done = f32[8,128,32]{1,2,0:T(8,128)} async-done(((f32[8,128,32]{1,2,0:T(8,128)}), f32[8,128,32]{1,2,0:T(8,128)}) %all-reduce.4.cloned.1.call-update) | async-done | bytes 131088 | tf_op jit(solution)/shard_map/pmax | solution.py:73
  475.0 8.4 %mul.66 = f32[8,128,32,128]{3,2,1,0:T(8,128)} broadcast(f32[8,128,32]{2,1,0:T(8,128)S(1)} %copy.37), dimensions={0,1,2} | broadcast | bytes 16908288 | tf_op jit(solution)/shard_map/mul | solution.py:75
  483.4 18.2 %mul.67 = f32[8,128,4096]{2,1,0:T(8,128)} reshape(f32[8,128,32,128]{3,2,1,0:T(8,128)} %mul.66) | data formatting | bytes 33554432 | tf_op jit(solution)/shard_map/mul | solution.py:75
  501.6 17.8 %mul.68 = f32[8,128,4096]{2,1,0:T(8,128)} multiply(f32[8,128,4096]{2,1,0:T(8,128)} %get-tuple-element.54, f32[8,128,4096]{2,1,0:T(8,128)} %mul.67) | non-fusion elementwise | flops 4194304 | bytes 50331648 | tf_op jit(solution)/shard_map/mul | solution.py:75
  523.0 211.3 %all-reduce.6.cloned.1.call-done = (f32[8,128,32]{1,2,0:T(8,128)}, f32[8,128,4096]{2,1,0:T(8,128)}) async-done(((f32[8,128,32]{1,2,0:T(8,128)}, f32[8,128,4096]{2,1,0:T(8,128)}), (f32[8,128,32]{1,2,0:T(8,128)}, f32[8,128,4096]{2,1,0:T(8,128)})) %all-reduce.6.cloned.1.call-update) | async-done | bytes 16908304 | tf_op jit(solution)/shard_map/psum | solution.py:86
  (126 shorter events, 146.1 us)
Async XLA Ops:
  6.5 512.9 %copy-start = (bf16[1024,1024]{1,0:T(8,128)(2,1)S(1)}, bf16[1024,1024]{1,0:T(8,128)(2,1)}, u32[]{:S(2)}) copy-start(bf16[1024,1024]{1,0:T(8,128)(2,1)} %param.12) | copy-start | bytes 6291460
  6.5 72.5 %all-gather.2.cloned.1.call-start = ((), (), s32[]{:S(2)}) async-start(), calls=%async_computation.1 | async-start | bytes 8912896 | tf_op jit(solution)/shard_map/all_gather | solution.py:68
  26.5 446.7 %all-reduce.4.cloned.1.call-start = ((), (), s32[]{:S(2)}) async-start(), calls=%async_computation.2 | async-start | bytes 262144 | tf_op jit(solution)/shard_map/pmax | solution.py:73
  26.6 64.9 %copy-start.4 = (s32[8]{0:T(128)S(1)}, s32[8]{0:T(128)}, u32[]{:S(2)}) copy-start(s32[8]{0:T(128)} %param.14) | copy-start | bytes 100
  99.6 3.2 copy-start.1
  129.7 3.2 copy-start.1
  159.8 3.2 copy-start.1
  189.9 3.2 copy-start.1
  220.0 3.2 copy-start.1
  250.1 3.2 copy-start.1
  280.2 3.2 copy-start.1
  310.4 3.2 copy-start.1
  332.4 401.9 %all-reduce.6.cloned.1.call-start = ((), (), s32[]{:S(2)}) async-start(), calls=%async_computation.3 | async-start | bytes 33816576 | tf_op jit(solution)/shard_map/psum | solution.py:86
  519.4 0.7 copy-start.3
  519.4 1.3 copy-start.2
Sparse Core Ops, SparseCore 0:
  26.6 52.3 all-gather.1
  332.5 140.5 all-reduce.3
  519.6 214.6 all-reduce.5
where the time goes:
time: 747 us; the launch traced here: 744 us
  waiting for transfers between devices  404 us (54%)
  local copies, waits for them, and re-layouts  179 us (24%)
  matrix products  82.9 us (11%)
  other arithmetic  46.2 us (6%)
  blocking collectives  17.5 us (2%)
  between operations  13.2 us (2%)
    psum x1, waiting for transfers between devices, body(): numer, total = lax.psum((weighted, mass), ('row', 'col'))  211 us
    pmax x1, waiting for transfers between devices, body(): peak_all = lax.pmax(peak_part, ('row', 'col'))  141 us
    dynamic_slice x48, local copies, waits for them, and re-layouts, cache_partials(): return lax.map(one_user, (whole, key_cache, value_cache, lengths))  57.7 us
    dot_general x8, matrix products, one_user(): jnp.einsum('kwgl,lkd->wkgd', weight.astype(jnp.bfloat16), v_heads, prefer...  57.5 us
    dynamic_update_slice x24, local copies, waits for them, and re-layouts, cache_partials(): return lax.map(one_user, (whole, key_cache, value_cache, lengths))  53.1 us
    all_gather x1, waiting for transfers between devices, body(): whole = lax.all_gather(whole, 'row', axis=1, tiled=True)  52.4 us
    mul x2, local copies, waits for them, and re-layouts, body(): numer_part.reshape(users, -1, HQ, HD) * factor[..., None]  26.6 us
    while x16, local copies, waits for them, and re-layouts  25.8 us
  transfers between devices with their start and end apart: 3, of which 3 were waited for; matrix products, arithmetic and copies ran while one was open for 0% of the time, Pallas kernels for 0%

commit v1 on v0

--- a/solution.py
+++ b/solution.py
@@ -83,7 +83,7 @@
             picked, col_at * heads_part * per_head, heads_part * per_head, 2
         )
 
-    numer, total = lax.psum((weighted, mass), ("row", "col"))
+    numer, total = lax.psum(lax.psum((weighted, mass), "row"), "col")
     numer = local_part(numer, HD)
     total = local_part(total, 1)
     peak = local_part(peak_all, 1)

time: 747 us -> 1400 us (1.87)
  waiting for transfers between devices: 404 us -> 1050 us
    psum x1 -> x2, waiting for transfers between devices: 211 us -> 856 us  [body(): numer, total = lax.psum(lax.psum((weighted, mass), 'row'), 'col')]
  transfers between devices with their start and end apart: 3 -> 4, of which waited for: 3 -> 4; matrix products, arithmetic and copies ran while one was open for 0% -> 0% of each run, Pallas kernels for 0% -> 0%
where the time goes in v1:
time: 1400 us; the launch traced here: 1390 us
  waiting for transfers between devices  1050 us (75%)
  local copies, waits for them, and re-layouts  179 us (13%)
  matrix products  83 us (6%)
  other arithmetic  46.6 us (3%)
  blocking collectives  17.5 us (1%)
    psum x2, waiting for transfers between devices, body(): numer, total = lax.psum(lax.psum((weighted, mass), 'row'), 'col')  856 us
    pmax x1, waiting for transfers between devices, body(): peak_all = lax.pmax(peak_part, ('row', 'col'))  141 us
    dynamic_slice x48, local copies, waits for them, and re-layouts, cache_partials(): return lax.map(one_user, (whole, key_cache, value_cache, lengths))  57.8 us
    dot_general x8, matrix products, one_user(): jnp.einsum('kwgl,lkd->wkgd', weight.astype(jnp.bfloat16), v_heads, prefer...  57.6 us
    dynamic_update_slice x24, local copies, waits for them, and re-layouts, cache_partials(): return lax.map(one_user, (whole, key_cache, value_cache, lengths))  53.3 us
    all_gather x1, waiting for transfers between devices, body(): whole = lax.all_gather(whole, 'row', axis=1, tiled=True)  52.4 us
  transfers between devices with their start and end apart: 4, of which 4 were waited for; matrix products, arithmetic and copies ran while one was open for 0% of the time, Pallas kernels for 0%

profile of v1, /device:TPU:1, one launch (start us, length us, event | category | flops | bytes accessed | tf_op | source)
XLA Modules:
  0.0 1389.3 jit_solution(17527837631499246619)
XLA Ops:
  7.6 17.5 %all_to_all.5 = bf16[8,8,8,512]{3,2,1,0:T(8,128)(2,1)S(1)} all-to-all(bf16[8,8,8,512]{3,2,1,0:T(8,128)(2,1)S(1)} %broadcast_in_dim.46), channel_id=1, replica_groups=mesh['row'=16,'col'=8] {'col'}, dimensions={0} | all-to-all | bytes 1048576 | tf_op jit(solution)/shard_map/all_to_all | solution.py:19
  26.6 52.4 %all-gather.2.cloned.1.call-done = bf16[8,128,4096]{2,0,1:T(8,128)(2,1)} async-done(((bf16[8,8,4096]{2,0,1:T(8,128)(2,1)}), bf16[8,128,4096]{2,0,1:T(8,128)(2,1)}) %all-gather.2.cloned.1.call-update) | async-done | bytes 8388624 | tf_op jit(solution)/shard_map/all_gather | solution.py:68
  79.0 12.5 copy.35
  91.5 241.6 %while.14 = (s32[]{:T(128)}, f32[8,128,4096]{2,1,0:T(8,128)}, f32[8,128,32]{1,2,0:T(8,128)}, f32[8,128,32]{1,2,0:T(8,128)S(1)}, bf16[8,512,1024]{2,1,0:T(8,128)(...) while((s32[]{:T(128)}, f32[8,128,4096]{2,1,0:T(8,128)}, ...), condition=%wide.region_3.4_spmd, body=%wide.region_0.3_spmd.sunk | while | flops 1100997632 | bytes 82971808 | solution.py:58
  99.7 3.2 copy-done.1
  108.5 7.2 fusion.46
  118.6 3.1 constant_dynamic-update-slice_fusion.2
  129.9 3.2 copy-done.1
  138.7 7.2 fusion.46
  160.1 3.2 copy-done.1
  168.8 7.2 fusion.46
  179.0 3.1 constant_dynamic-update-slice_fusion.2
  190.3 3.2 copy-done.1
  199.0 7.2 fusion.46
  209.2 3.1 constant_dynamic-update-slice_fusion.2
  220.5 3.2 copy-done.1
  229.3 7.2 fusion.46
  239.4 3.2 constant_dynamic-update-slice_fusion.2
  250.7 3.2 copy-done.1
  259.5 7.2 fusion.46
  269.6 3.1 constant_dynamic-update-slice_fusion.2
  280.9 3.2 copy-done.1
  289.7 7.2 fusion.46
  299.8 3.1 constant_dynamic-update-slice_fusion.2
  311.1 3.2 copy-done.1
  319.9 7.2 fusion.46
  333.2 140.7 %all-reduce.6.cloned.1.call-done = f32[8,128,32]{1,2,0:T(8,128)} async-done(((f32[8,128,32]{1,2,0:T(8,128)}), f32[8,128,32]{1,2,0:T(8,128)}) %all-reduce.6.cloned.1.call-update) | async-done | bytes 131088 | tf_op jit(solution)/shard_map/pmax | solution.py:73
  475.8 8.4 mul.66
  484.2 18.2 %mul.67 = f32[8,128,4096]{2,1,0:T(8,128)} reshape(f32[8,128,32,128]{3,2,1,0:T(8,128)} %mul.66) | data formatting | bytes 33554432 | tf_op jit(solution)/shard_map/mul | solution.py:75
  502.3 17.9 %mul.68 = f32[8,128,4096]{2,1,0:T(8,128)} multiply(f32[8,128,4096]{2,1,0:T(8,128)} %get-tuple-element.54, f32[8,128,4096]{2,1,0:T(8,128)} %mul.67) | non-fusion elementwise | flops 4194304 | bytes 50331648 | tf_op jit(solution)/shard_map/mul | solution.py:75
  520.3 193.5 %all-reduce.8.cloned.1.call-done = (f32[8,128,32]{1,2,0:T(8,128)}, f32[8,128,4096]{2,1,0:T(8,128)}) async-done(((f32[8,128,32]{1,2,0:T(8,128)}, f32[8,128,4096]{2,1,0:T(8,128)}), (f32[8,128,32]{1,2,0:T(8,128)}, f32[8,128,4096]{2,1,0:T(8,128)})) %all-reduce.8.cloned.1.call-update) | async-done | bytes 16908304 | tf_op jit(solution)/shard_map/psum | solution.py:86
  717.4 662.5 %all-reduce.10.cloned.1.call-done = (f32[8,128,32]{1,2,0:T(8,128)}, f32[8,128,4096]{2,1,0:T(8,128)}) async-done(((f32[8,128,32]{1,2,0:T(8,128)}, f32[8,128,4096]{2,1,0:T(8,128)}), (f32[8,128,32]{1,2,0:T(8,128)}, f32[8,128,4096]{2,1,0:T(8,128)})) %all-reduce.10.cloned.1.call-update) | async-done | bytes 16908304 | tf_op jit(solution)/shard_map/psum | solution.py:86
  (129 shorter events, 150.0 us)
Async XLA Ops:
  6.5 707.3 %copy-start = (bf16[1024,1024]{1,0:T(8,128)(2,1)S(1)}, bf16[1024,1024]{1,0:T(8,128)(2,1)}, u32[]{:S(2)}) copy-start(bf16[1024,1024]{1,0:T(8,128)(2,1)} %param.12) | copy-start | bytes 6291460
  6.5 72.5 %all-gather.2.cloned.1.call-start = ((), (), s32[]{:S(2)}) async-start(), calls=%async_computation.1 | async-start | bytes 8912896 | tf_op jit(solution)/shard_map/all_gather | solution.py:68
  26.5 447.4 %all-reduce.6.cloned.1.call-start = ((), (), s32[]{:S(2)}) async-start(), calls=%async_computation.2 | async-start | bytes 262144 | tf_op jit(solution)/shard_map/pmax | solution.py:73
  26.6 64.9 %copy-start.4 = (s32[8]{0:T(128)S(1)}, s32[8]{0:T(128)}, u32[]{:S(2)}) copy-start(s32[8]{0:T(128)} %param.14) | copy-start | bytes 100
  99.7 3.2 copy-start.1
  129.9 3.2 copy-start.1
  160.1 3.2 copy-start.1
  190.3 3.2 copy-start.1
  220.5 3.2 copy-start.1
  250.7 3.2 copy-start.1
  280.9 3.2 copy-start.1
  311.1 3.2 copy-start.1
  333.2 380.7 %all-reduce.8.cloned.1.call-start = ((), (), s32[]{:S(2)}) async-start(), calls=%async_computation.3 | async-start | bytes 33816576 | tf_op jit(solution)/shard_map/psum | solution.py:86
  520.2 859.7 %all-reduce.10.cloned.1.call-start = ((), (), s32[]{:S(2)}) async-start(), calls=%async_computation.4 | async-start | bytes 33816576 | tf_op jit(solution)/shard_map/psum | solution.py:86
  713.8 0.7 copy-start.3
  713.8 1.3 copy-start.2
Sparse Core Ops, SparseCore 0:
  26.6 52.3 all-gather.1
  333.3 140.5 all-reduce.5
  520.3 193.4 all-reduce.7
  716.7 663.1 all-reduce.9
